TPU v7x, 32 devices: a whole 2x2x4 slice. The times are simulated.
32 devices in a mesh: dp: 2 (over x), cluster: 16 (over z, y, core).
Axes of the slice: x: 2, y: 2, z: 4, core: 2. Of those that a mesh axis runs over, the one named last changes fastest.
Arguments:
- queries: bfloat16 [4096, 768], P(('dp', 'cluster')), may hold values from -6 to 6
- shortlist: int32 [4096, 8], P(('dp', 'cluster')), may hold values from 0 to 15, all different within a row; in each aligned block of 128 rows (0 to 127, 128 to 255, ...) at most 128 rows name the same one
- positives: int32 [4096, 8], P(('dp', 'cluster')), may hold values from 0 to 255
- weights: bfloat16 [16, 256, 768], P('cluster'), may hold values from -0.21875 to 0.21875
- first_moment: float32 [16, 256, 768], P('cluster'), may hold values from -24 to 24
- second_moment: float32 [16, 256, 768], P('cluster'), may hold values from 0.5 to 50
Outputs:
- new_weights: bfloat16 [16, 256, 768], P('cluster')
- new_first: float32 [16, 256, 768], P('cluster')
- new_second: float32 [16, 256, 768], P('cluster')
- query_grad: bfloat16 [4096, 768], P(('dp', 'cluster'))
Inputs may be any that keep to these rules, and one draw needn't show every extreme that they name: `shortlist`: each row names 8 different clusters. In the rows of one device no cluster is named by more than 128 rows, a bound that some block reaches of them.
All inputs are finite; a program needn't handle non-finite values.
Results may differ from a plain program's by a relative error of at most 0.0085.
Values may be sent and summed in bfloat16 or wider, within the bound.
No kernel may reach another device: no remote copies, remote signals or barrier semaphores. Data moves between devices by JAX's collectives and lax.ppermute only.
A program may use at most 64 MiB of HBM per device.

v0:
```python
import jax
import jax.numpy as jnp
from jax import lax
from jax.sharding import PartitionSpec as P

beta_one = 0.9
beta_two = 0.999
learn_rate = 0.01
adam_eps = 1e-08
adam_step = 10.0


def adam_update(cluster_weights, first_moment, second_moment, gradient):
    first_new = beta_one * first_moment + (1.0 - beta_one) * gradient
    second_new = beta_two * second_moment + (1.0 - beta_two) * gradient * gradient
    first_hat = first_new / (1.0 - beta_one**adam_step)
    second_hat = second_new / (1.0 - beta_two**adam_step)
    stepped = cluster_weights.astype(jnp.float32) - learn_rate * first_hat / (
        jnp.sqrt(second_hat) + adam_eps
    )
    return (stepped.astype(jnp.bfloat16), first_new, second_new)


def owner_work(arrived_rows, arrived_labels, cluster_rows):
    label_ids = jnp.arange(cluster_rows.shape[0], dtype=jnp.int32)
    scores = lax.dot_general(
        arrived_rows, cluster_rows, (((1,), (1,)), ((), ())), preferred_element_type=jnp.float32
    )
    target = (arrived_labels[:, None] == label_ids[None, :]).astype(jnp.float32)
    coefficient = (jax.nn.sigmoid(scores) - target).astype(jnp.bfloat16)
    gradient = lax.dot_general(
        coefficient, arrived_rows, (((0,), (0,)), ((), ())), preferred_element_type=jnp.float32
    )
    visit_grad = jnp.dot(coefficient, cluster_rows, preferred_element_type=jnp.float32).astype(
        jnp.bfloat16
    )
    return (gradient, visit_grad)


def on_device(queries, shortlist, positives, weights, first_moment, second_moment):
    owners = lax.axis_size("cluster")
    rows_dev, fanout = shortlist.shape
    feature_dim = queries.shape[1]
    capacity = min(rows_dev, 2 * rows_dev * fanout // owners)
    visits = shortlist.reshape(-1)
    labels = positives.reshape(-1)
    onehot = (visits[:, None] == jnp.arange(owners, dtype=jnp.int32)[None, :]).astype(jnp.int32)
    visit_rank = jnp.sum((jnp.cumsum(onehot, axis=0) - onehot) * onehot, axis=1)
    slot_index = visits * capacity + visit_rank
    slot_visit = (
        jnp.full((owners * capacity,), -1, jnp.int32)
        .at[slot_index]
        .set(jnp.arange(visits.shape[0], dtype=jnp.int32))
    )
    filled = slot_visit >= 0
    clamped = jnp.maximum(slot_visit, 0)
    send_rows = jnp.where(filled[:, None], queries[clamped // fanout], jnp.zeros((), queries.dtype))
    send_labels = jnp.where(filled, labels[clamped], -1)
    cluster_rows = weights[0]
    arrived_rows, arrived_labels = (
        lax.all_to_all(
            send_rows.reshape(owners, capacity, feature_dim),
            "cluster",
            split_axis=0,
            concat_axis=0,
            tiled=True,
        ),
        lax.all_to_all(
            send_labels.reshape(owners, capacity),
            "cluster",
            split_axis=0,
            concat_axis=0,
            tiled=True,
        ),
    )
    gradient, visit_grad = owner_work(
        arrived_rows.reshape(-1, feature_dim), arrived_labels.reshape(-1), cluster_rows
    )
    returned = lax.all_to_all(
        visit_grad.reshape(owners, capacity, feature_dim),
        "cluster",
        split_axis=0,
        concat_axis=0,
        tiled=True,
    )
    per_visit = returned.reshape(-1, feature_dim)[slot_index].astype(jnp.float32)
    query_grad = jnp.sum(per_visit.reshape(rows_dev, fanout, feature_dim), axis=1).astype(
        jnp.bfloat16
    )
    summed = lax.psum(gradient.astype(jnp.bfloat16), "dp").astype(jnp.float32)
    new_weights, new_first, new_second = adam_update(
        cluster_rows, first_moment[0], second_moment[0], summed
    )
    return (new_weights[None], new_first[None], new_second[None], query_grad)


def solution(mesh):
    in_specs = (
        P(("dp", "cluster"), None),
        P(("dp", "cluster"), None),
        P(("dp", "cluster"), None),
        P("cluster", None, None),
        P("cluster", None, None),
        P("cluster", None, None),
    )
    out_specs = (
        P("cluster", None, None),
        P("cluster", None, None),
        P("cluster", None, None),
        P(("dp", "cluster"), None),
    )
    return jax.shard_map(
        on_device, mesh=mesh, in_specs=in_specs, out_specs=out_specs, check_vma=False
    )
```

profile of v0, /device:TPU:13, one launch (start us, length us, event | category | flops | bytes accessed | tf_op | source)
XLA Modules:
  0.0 218.1 jit_solution(6871849412178040356)
XLA Ops:
  7.2 0.7 broadcast_multiply_fusion
  7.9 0.8 copy.13
  8.7 0.1 eq.44
  8.8 0.1 eq.40
  8.9 0.1 copy.12
  9.0 0.1 mul.63
  9.1 4.5 %reduce-window.6 = s32[16,8,128]{2,1,0:T(8,128)S(1)} reduce-window(s32[16,8,128]{2,1,0:T(8,128)S(1)} %fusion.15, s32[]{:T(128)} %constant.23.clone.1), window={size=1x1x128 pad=0_0x0_0x127_0}, to_apply=%region_0.0 | reduce-window | flops 2080768 | bytes 131076 | tf_op jit(solution)/shard_map/reduce-window
  13.6 0.1 slice.14
  13.7 0.1 copy.15
  13.9 0.1 copy.16
  13.9 0.1 broadcast_add_fusion
  14.1 4.3 %scatter_custom_fusion = s32[2048]{0:T(1024)S(1)} fusion(s32[1024]{0:T(1024)S(1)} %bitcast.72, s32[1024]{0:T(1024)S(1)} %iota.15, s32[]{:T(128)} %constant.20.clone.1), kind=kCustom, calls=%fused_computation.43 | custom fusion | bytes 8196 | tf_op jit(solution)/shard_map/scatter | solution.py:53
  18.4 0.8 copy.17
  19.2 0.1 reshape.88
  19.3 8.6 %gather_fusion.1 = s32[2048]{0:T(1024)S(1)} fusion(s32[1024]{0:T(1024)S(1)} %reshape.88, s32[2048]{0:T(1024)S(1)} %maximum_clamp_fusion), kind=kCustom, calls=%fused_computation.1 | custom fusion | bytes 24576 | tf_op jit(solution)/shard_map/gather | solution.py:58
  27.9 0.6 broadcast_select_fusion.1
  28.5 6.5 %all-to-all-start.1 = ((s32[16,1,128]{2,1,0:T(1,128)}), s32[16,1,128]{2,1,0:T(1,128)S(1)}, u32[]{:S(2)}, u32[]{:S(2)}) async-start(s32[16,1,128]{2,1,0:T(1,128)} %bitcast.9), calls=%async_computation.1 | async-start | bytes 16384 | tf_op jit(solution)/shard_map/all_to_all | solution.py:68
  35.0 9.4 %gather_fusion = bf16[2048,768]{1,0:T(8,128)(2,1)} fusion(bf16[128,768]{1,0:T(8,128)(2,1)S(1)} %copy-done, s32[2048]{0:T(1024)S(1)} %get-tuple-element.9), kind=kCustom, calls=%fused_computation | custom fusion | bytes 6299648 | tf_op jit(solution)/shard_map/gather | solution.py:57
  44.4 2.1 broadcast_select_fusion
  46.5 75.7 %all_to_all.19 = bf16[16,128,768]{2,1,0:T(8,128)(2,1)S(1)} all-to-all(bf16[16,128,768]{2,1,0:T(8,128)(2,1)S(1)} %broadcast_select_fusion), channel_id=1, replica_groups=mesh['dp'=2,'cluster'=16] {'cluster'}, dimensions={0} | all-to-all | bytes 6291456 | tf_op jit(solution)/shard_map/all_to_all | solution.py:61
  122.2 1.7 copy-done.2
  123.9 1.3 fusion.4
  125.3 2.7 %convolution_convert_fusion = bf16[2048,768]{1,0:T(8,128)(2,1)} fusion(bf16[2048,256]{1,0:T(8,128)(2,1)S(1)} %fusion.4, bf16[1,256,768]{2,1,0:T(8,128)(2,1)S(1)} %copy-done.3), kind=kOutput, calls=%fused_computation.4 | convolution fusion | flops 806879232 | bytes 4587520 | tf_op jit(solution)/shard_map/dot_general | solution.py:34
  127.9 5.1 %all-to-all-start.2 = ((bf16[16,128,768]{2,1,0:T(8,128)(2,1)}), bf16[16,128,768]{2,1,0:T(8,128)(2,1)S(1)}, u32[]{:S(2)}, u32[]{:S(2)}) async-start(bf16[16,128,768]{2,1,0:T(8,128)(2,1)} %bitcast.65), calls=%async_computation.2 | async-start | bytes 6291456 | tf_op jit(solution)/shard_map/all_to_all | solution.py:79
  133.0 0.0 all-reduce.2.cloned.1.call-start
  133.1 4.0 %convolution_convert_fusion.1 = bf16[256,768]{1,0:T(8,128)(2,1)} fusion(bf16[2048,256]{1,0:T(8,128)(2,1)} %copy-done.1, bf16[2048,768]{1,0:T(8,128)(2,1)} %bitcast.68), kind=kOutput, calls=%fused_computation.14 | convolution fusion | flops 805502976 | bytes 4587520 | tf_op jit(solution)/shard_map/dot_general | solution.py:31
  137.1 0.0 all-reduce.2.cloned.1.call-update
  137.1 26.4 %all-reduce.2.cloned.1.call-done = bf16[256,768]{1,0:T(8,128)(2,1)} async-done(((bf16[256,768]{1,0:T(8,128)(2,1)}), bf16[256,768]{1,0:T(8,128)(2,1)}) %all-reduce.2.cloned.1.call-update) | async-done | bytes 393232 | tf_op jit(solution)/shard_map/psum | solution.py:90
  163.5 3.4 %fusion.8 = (f32[1,256,768]{2,1,0:T(8,128)}, bf16[1,256,768]{2,1,0:T(8,128)(2,1)}, f32[1,256,768]{2,1,0:T(8,128)}) fusion(bf16[256,768]{1,0:T(8,128)(2,1)} %all-reduce.2.cloned.1.call-done, f32[1,256,768]{2,1,0:T(8,128)} %param.11, f32[1,256,768]{2,1,0:T(8,128)} %param.10, bf16[1,256,768]{2,1,0:T(8,128)(2,1)} %param.9), kind=kLoop, calls=%fused_computation.21 | loop fusion | flops 2949120 | bytes 4325376 | tf_op jit(solution)/shard_map/broadcast_in_dim | solution.py:94
  166.9 36.0 %all-to-all-done.2 = bf16[16,128,768]{2,1,0:T(8,128)(2,1)S(1)} async-done(((bf16[16,128,768]{2,1,0:T(8,128)(2,1)}), bf16[16,128,768]{2,1,0:T(8,128)(2,1)S(1)}, u32[]{:S(2)}, u32[]{:S(2)}) %all-to-all-start.2) | async-done | bytes 3145760 | tf_op jit(solution)/shard_map/all_to_all | solution.py:79
  202.9 5.2 %gather_fusion.2 = bf16[1024,768]{1,0:T(8,128)(2,1)} fusion(bf16[2048,768]{1,0:T(8,128)(2,1)S(1)} %bitcast.64, s32[1024]{0:T(1024)S(1)} %broadcast_clamp_fusion), kind=kCustom, calls=%fused_computation.2 | custom fusion | bytes 3149824 | tf_op jit(solution)/shard_map/gather | solution.py:86
  208.1 3.1 %bitcast_reduce_fusion = bf16[128,768]{1,0:T(8,128)(2,1)} fusion(bf16[1024,768]{1,0:T(8,128)(2,1)} %gather_fusion.2), kind=kLoop, calls=%fused_computation.13 | loop fusion | flops 688128 | bytes 1769472 | tf_op jit(solution)/shard_map/reduce_sum | solution.py:87
  (16 shorter events, 0.1 us)
Async XLA Ops:
  7.2 27.9 %copy-start = (bf16[128,768]{1,0:T(8,128)(2,1)S(1)}, bf16[128,768]{1,0:T(8,128)(2,1)}, u32[]{:S(2)}) copy-start(bf16[128,768]{1,0:T(8,128)(2,1)} %param.6) | copy-start | bytes 589828
  28.5 18.0 %all-to-all-start.1 = ((s32[16,1,128]{2,1,0:T(1,128)}), s32[16,1,128]{2,1,0:T(1,128)S(1)}, u32[]{:S(2)}, u32[]{:S(2)}) async-start(s32[16,1,128]{2,1,0:T(1,128)} %bitcast.9), calls=%async_computation.1 | async-start | bytes 16384 | tf_op jit(solution)/shard_map/all_to_all | solution.py:68
  46.5 77.4 %copy-start.3 = (bf16[1,256,768]{2,1,0:T(8,128)(2,1)S(1)}, bf16[1,256,768]{2,1,0:T(8,128)(2,1)}, u32[]{:S(2)}) copy-start(bf16[1,256,768]{2,1,0:T(8,128)(2,1)} %param.9) | copy-start | bytes 1179652
  122.2 1.7 copy-start.2
  125.3 2.7 %copy-start.1 = (bf16[2048,256]{1,0:T(8,128)(2,1)}, bf16[2048,256]{1,0:T(8,128)(2,1)S(1)}, u32[]{:S(2)}) copy-start(bf16[2048,256]{1,0:T(8,128)(2,1)S(1)} %fusion.4) | copy-start | bytes 3145732
  127.9 75.0 %all-to-all-start.2 = ((bf16[16,128,768]{2,1,0:T(8,128)(2,1)}), bf16[16,128,768]{2,1,0:T(8,128)(2,1)S(1)}, u32[]{:S(2)}, u32[]{:S(2)}) async-start(bf16[16,128,768]{2,1,0:T(8,128)(2,1)} %bitcast.65), calls=%async_computation.2 | async-start | bytes 6291456 | tf_op jit(solution)/shard_map/all_to_all | solution.py:79
  133.0 30.4 %all-reduce.2.cloned.1.call-start = ((), (), s32[]{:S(2)}) async-start(), calls=%async_computation.3 | async-start | bytes 786432 | tf_op jit(solution)/shard_map/psum | solution.py:90
Sparse Core Ops, SparseCore 0:
  137.2 26.2 all-reduce.1
where the time goes:
time: 219 us; the launch traced here: 218 us
  blocking collectives  75.7 us (35%)
  waiting for transfers between devices  62.4 us (28%)
  local copies, waits for them, and re-layouts  31.5 us (14%)
  other arithmetic  14.7 us (7%)
  between operations  14.2 us (6%)
  starting transfers between devices  11.7 us (5%)
  matrix products  7.95 us (4%)
    all_to_all x1, blocking collectives, on_device(): lax.all_to_all(send_rows.reshape(owners, capacity, feature_dim), 'cluster...  75.7 us
    all_to_all x1, waiting for transfers between devices, on_device(): lax.all_to_all(visit_grad.reshape(owners, capacity, feature_dim), 'cluste...  36 us
    psum x1, waiting for transfers between devices, on_device(): summed = lax.psum(gradient.astype(jnp.bfloat16), 'dp').astype(jnp.float32)  26.4 us
    gather x1, local copies, waits for them, and re-layouts, on_device(): queries[clamped // fanout]  9.38 us
    gather x1, local copies, waits for them, and re-layouts, on_device(): send_labels = jnp.where(filled, labels[clamped], -1)  8.58 us
    all_to_all x1, starting transfers between devices, on_device(): lax.all_to_all(send_labels.reshape(owners, capacity), 'cluster', split_ax...  6.52 us
    gather x1, local copies, waits for them, and re-layouts, on_device(): returned.reshape(-1, feature_dim)[slot_index].astype(jnp.float32)  5.21 us
    all_to_all x1, starting transfers between devices, on_device(): lax.all_to_all(visit_grad.reshape(owners, capacity, feature_dim), 'cluste...  5.1 us
  transfers between devices with their start and end apart: 3, of which 2 were waited for; matrix products, arithmetic and copies ran while one was open for 9% of the time, Pallas kernels for 0%

commit v1 on v0

--- a/solution.py
+++ b/solution.py
@@ -8,6 +8,11 @@
 learn_rate = 0.01
 adam_eps = 1e-08
 adam_step = 10.0
+
+
+def summed_here(array, mesh_axis):
+    parts = lax.all_gather(array, mesh_axis)
+    return jnp.sum(parts, axis=0)
 
 
 def adam_update(cluster_weights, first_moment, second_moment, gradient):
@@ -87,7 +92,7 @@
     query_grad = jnp.sum(per_visit.reshape(rows_dev, fanout, feature_dim), axis=1).astype(
         jnp.bfloat16
     )
-    summed = lax.psum(gradient.astype(jnp.bfloat16), "dp").astype(jnp.float32)
+    summed = summed_here(gradient.astype(jnp.bfloat16), "dp").astype(jnp.float32)
     new_weights, new_first, new_second = adam_update(
         cluster_rows, first_moment[0], second_moment[0], summed
     )

time: 219 us -> 205 us (0.936)
  between operations: 14.2 us -> 0.77 us
  waiting for transfers between devices: 62.4 us -> 50.3 us
  blocking collectives: 75.7 us -> 86.7 us
    psum x1 -> x0, waiting for transfers between devices: 26.4 us -> none  [on_device(): summed = lax.psum(gradient.astype(jnp.bfloat16), 'dp').astype(jnp.float32)]
    all_to_all x1, waiting for transfers between devices: 36 us -> 50.3 us  [on_device(): lax.all_to_all(visit_grad.reshape(owners, capacity, feature_dim), 'cluste...]
    all_gather x0 -> x1, blocking collectives: none -> 11 us  [summed_here(): parts = lax.all_gather(array, mesh_axis)]
    broadcast_in_dim x1 -> x0, other arithmetic: 3.42 us -> none  [on_device(): return (new_weights[None], new_first[None], new_second[None], query_grad)]
    convert_element_type x0 -> x1, other arithmetic: none -> 3.23 us  [adam_update(): return (stepped.astype(jnp.bfloat16), first_new, second_new)]
  transfers between devices with their start and end apart: 3 -> 2, of which waited for: 2 -> 1; matrix products, arithmetic and copies ran while one was open for 9% -> 10% of each run, Pallas kernels for 0% -> 0%
where the time goes in v1:
time: 205 us
  blocking collectives  86.7 us (42%)
  waiting for transfers between devices  50.3 us (25%)
  local copies, waits for them, and re-layouts  31.5 us (15%)
  other arithmetic  16.6 us (8%)
  starting transfers between devices  11.6 us (6%)
  matrix products  7.2 us (4%)
    all_to_all x1, blocking collectives, on_device(): lax.all_to_all(send_rows.reshape(owners, capacity, feature_dim), 'cluster...  75.7 us
    all_to_all x1, waiting for transfers between devices, on_device(): lax.all_to_all(visit_grad.reshape(owners, capacity, feature_dim), 'cluste...  50.3 us
    all_gather x1, blocking collectives, summed_here(): parts = lax.all_gather(array, mesh_axis)  11 us
    gather x1, local copies, waits for them, and re-layouts, on_device(): queries[clamped // fanout]  9.38 us
    gather x1, local copies, waits for them, and re-layouts, on_device(): send_labels = jnp.where(filled, labels[clamped], -1)  8.58 us
    all_to_all x1, starting transfers between devices, on_device(): lax.all_to_all(send_labels.reshape(owners, capacity), 'cluster', split_ax...  6.52 us
    gather x1, local copies, waits for them, and re-layouts, on_device(): returned.reshape(-1, feature_dim)[slot_index].astype(jnp.float32)  5.21 us
    all_to_all x1, starting transfers between devices, on_device(): lax.all_to_all(visit_grad.reshape(owners, capacity, feature_dim), 'cluste...  5.1 us
  transfers between devices with their start and end apart: 2, of which 1 were waited for; matrix products, arithmetic and copies ran while one was open for 10% of the time, Pallas kernels for 0%

profile of v1, /device:TPU:13, one launch (start us, length us, event | category | flops | bytes accessed | tf_op | source)
XLA Modules:
  0.0 204.7 jit_solution(3301118282861082933)
XLA Ops:
  0.6 0.0 copy-start
  0.6 0.7 broadcast_multiply_fusion
  1.4 0.8 copy.13
  2.2 0.1 eq.44
  2.3 0.1 eq.40
  2.3 0.1 copy.12
  2.4 0.1 mul.85
  2.6 4.5 %reduce-window.6 = s32[16,8,128]{2,1,0:T(8,128)S(1)} reduce-window(s32[16,8,128]{2,1,0:T(8,128)S(1)} %fusion.12, s32[]{:T(128)} %constant.24.clone.1), window={size=1x1x128 pad=0_0x0_0x127_0}, to_apply=%region_0.0 | reduce-window | flops 2080768 | bytes 131076 | tf_op jit(solution)/shard_map/reduce-window
  7.1 0.1 slice.14
  7.2 0.1 copy.15
  7.3 0.1 copy.16
  7.4 0.1 broadcast_add_fusion
  7.6 4.3 %scatter_custom_fusion = s32[2048]{0:T(1024)S(1)} fusion(s32[1024]{0:T(1024)S(1)} %bitcast.55, s32[1024]{0:T(1024)S(1)} %iota.15, s32[]{:T(128)} %constant.21.clone.1), kind=kCustom, calls=%fused_computation.41 | custom fusion | bytes 8196 | tf_op jit(solution)/shard_map/scatter | solution.py:58
  11.9 0.8 copy.17
  12.7 0.1 reshape.107
  12.8 8.6 %gather_fusion.1 = s32[2048]{0:T(1024)S(1)} fusion(s32[1024]{0:T(1024)S(1)} %reshape.107, s32[2048]{0:T(1024)S(1)} %maximum_clamp_fusion), kind=kCustom, calls=%fused_computation.1 | custom fusion | bytes 24576 | tf_op jit(solution)/shard_map/gather | solution.py:63
  21.4 0.6 broadcast_select_fusion.1
  22.0 6.5 %all-to-all-start.1 = ((s32[16,1,128]{2,1,0:T(1,128)}), s32[16,1,128]{2,1,0:T(1,128)S(1)}, u32[]{:S(2)}, u32[]{:S(2)}) async-start(s32[16,1,128]{2,1,0:T(1,128)} %bitcast.8), calls=%async_computation.1 | async-start | bytes 16384 | tf_op jit(solution)/shard_map/all_to_all | solution.py:73
  28.5 9.4 %gather_fusion = bf16[2048,768]{1,0:T(8,128)(2,1)} fusion(bf16[128,768]{1,0:T(8,128)(2,1)S(1)} %copy-done, s32[2048]{0:T(1024)S(1)} %get-tuple-element.9), kind=kCustom, calls=%fused_computation | custom fusion | bytes 6299648 | tf_op jit(solution)/shard_map/gather | solution.py:62
  37.9 2.1 %broadcast_select_fusion = bf16[16,128,768]{2,1,0:T(8,128)(2,1)S(1)} fusion(bf16[16,128,768]{2,1,0:T(8,128)(2,1)} %bitcast.48, pred[16,128]{1,0:T(8,128)(4,1)S(1)} %bitcast.57), kind=kLoop, calls=%fused_computation.5 | loop fusion | flops 1572864 | bytes 6293504 | tf_op jit(solution)/shard_map/jit(_where)/select_n | solution.py:62
  40.0 75.7 %all_to_all.19 = bf16[16,128,768]{2,1,0:T(8,128)(2,1)S(1)} all-to-all(bf16[16,128,768]{2,1,0:T(8,128)(2,1)S(1)} %broadcast_select_fusion), channel_id=1, replica_groups=mesh['dp'=2,'cluster'=16] {'cluster'}, dimensions={0} | all-to-all | bytes 6291456 | tf_op jit(solution)/shard_map/all_to_all | solution.py:66
  115.7 1.7 copy-done.2
  117.4 1.3 fusion.4
  118.7 2.7 %convolution_convert_fusion = bf16[2048,768]{1,0:T(8,128)(2,1)} fusion(bf16[2048,256]{1,0:T(8,128)(2,1)S(1)} %fusion.4, bf16[1,256,768]{2,1,0:T(8,128)(2,1)S(1)} %copy-done.3), kind=kOutput, calls=%fused_computation.4 | convolution fusion | flops 806879232 | bytes 4587520 | tf_op jit(solution)/shard_map/dot_general | solution.py:39
  121.4 5.1 %all-to-all-start.2 = ((bf16[16,128,768]{2,1,0:T(8,128)(2,1)}), bf16[16,128,768]{2,1,0:T(8,128)(2,1)S(1)}, u32[]{:S(2)}, u32[]{:S(2)}) async-start(bf16[16,128,768]{2,1,0:T(8,128)(2,1)} %bitcast.47), calls=%async_computation.2 | async-start | bytes 6291456 | tf_op jit(solution)/shard_map/all_to_all | solution.py:84
  126.5 3.2 %convolution_convert_fusion.1 = bf16[256,768]{1,0:T(8,128)(2,1)S(1)} fusion(bf16[2048,256]{1,0:T(8,128)(2,1)} %copy-done.1, bf16[2048,768]{1,0:T(8,128)(2,1)} %bitcast.50), kind=kOutput, calls=%fused_computation.14 | convolution fusion | flops 805502976 | bytes 4587520 | tf_op jit(solution)/shard_map/dot_general | solution.py:36
  129.7 11.0 %all-gather = bf16[512,768]{1,0:T(8,128)(2,1)} all-gather(bf16[256,768]{1,0:T(8,128)(2,1)S(1)} %convolution_convert_fusion.1), channel_id=2, replica_groups=mesh['dp'=2,'cluster'=16] {'dp'}, dimensions={0}, use_global_device_ids=true | all-gather | bytes 1179648 | tf_op jit(solution)/shard_map/all_gather | solution.py:14
  140.8 2.1 %reduce_sum.37 = bf16[256,768]{1,0:T(8,128)(2,1)} reduce(bf16[2,256,768]{2,1,0:T(8,128)(2,1)} %bitcast.51, bf16[]{:T(256)} %constant.52.clone.1), dimensions={0}, to_apply=%region_4.5 | reduce | flops 196608 | bytes 1179650 | tf_op jit(solution)/shard_map/reduce_sum | solution.py:15
  142.9 3.2 %subtract_convert_fusion = (bf16[1,256,768]{2,1,0:T(8,128)(2,1)}, f32[1,256,768]{2,1,0:T(8,128)}, f32[1,256,768]{2,1,0:T(8,128)}) fusion(bf16[1,256,768]{2,1,0:T(8,128)(2,1)} %param.9, bf16[256,768]{1,0:T(8,128)(2,1)} %reduce_sum.37, f32[1,256,768]{2,1,0:T(8,128)} %param.10, f32[1,256,768]{2,1,0:T(8,128)} %param.11), kind=kLoop, calls=%fused_computation.20 | loop fusion | flops 2949120 | bytes 4325376 | tf_op jit(solution)/shard_map/convert_element_type | solution.py:26
  146.1 50.3 %all-to-all-done.2 = bf16[16,128,768]{2,1,0:T(8,128)(2,1)S(1)} async-done(((bf16[16,128,768]{2,1,0:T(8,128)(2,1)}), bf16[16,128,768]{2,1,0:T(8,128)(2,1)S(1)}, u32[]{:S(2)}, u32[]{:S(2)}) %all-to-all-start.2) | async-done | bytes 3145760 | tf_op jit(solution)/shard_map/all_to_all | solution.py:84
  196.4 5.2 %gather_fusion.2 = bf16[1024,768]{1,0:T(8,128)(2,1)} fusion(bf16[2048,768]{1,0:T(8,128)(2,1)S(1)} %bitcast.46, s32[1024]{0:T(1024)S(1)} %broadcast_clamp_fusion), kind=kCustom, calls=%fused_computation.2 | custom fusion | bytes 3149824 | tf_op jit(solution)/shard_map/gather | solution.py:91
  201.6 3.1 %bitcast_reduce_fusion = bf16[128,768]{1,0:T(8,128)(2,1)} fusion(bf16[1024,768]{1,0:T(8,128)(2,1)} %gather_fusion.2), kind=kLoop, calls=%fused_computation.13 | loop fusion | flops 688128 | bytes 1769472 | tf_op jit(solution)/shard_map/reduce_sum | solution.py:92
  (15 shorter events, 0.1 us)
Async XLA Ops:
  0.6 27.9 %copy-start = (bf16[128,768]{1,0:T(8,128)(2,1)S(1)}, bf16[128,768]{1,0:T(8,128)(2,1)}, u32[]{:S(2)}) copy-start(bf16[128,768]{1,0:T(8,128)(2,1)} %param.6) | copy-start | bytes 589828
  22.0 18.0 %all-to-all-start.1 = ((s32[16,1,128]{2,1,0:T(1,128)}), s32[16,1,128]{2,1,0:T(1,128)S(1)}, u32[]{:S(2)}, u32[]{:S(2)}) async-start(s32[16,1,128]{2,1,0:T(1,128)} %bitcast.8), calls=%async_computation.1 | async-start | bytes 16384 | tf_op jit(solution)/shard_map/all_to_all | solution.py:73
  40.0 77.4 %copy-start.3 = (bf16[1,256,768]{2,1,0:T(8,128)(2,1)S(1)}, bf16[1,256,768]{2,1,0:T(8,128)(2,1)}, u32[]{:S(2)}) copy-start(bf16[1,256,768]{2,1,0:T(8,128)(2,1)} %param.9) | copy-start | bytes 1179652
  115.7 1.7 copy-start.2
  118.7 2.7 %copy-start.1 = (bf16[2048,256]{1,0:T(8,128)(2,1)}, bf16[2048,256]{1,0:T(8,128)(2,1)S(1)}, u32[]{:S(2)}) copy-start(bf16[2048,256]{1,0:T(8,128)(2,1)S(1)} %fusion.4) | copy-start | bytes 3145732
  121.4 75.0 %all-to-all-start.2 = ((bf16[16,128,768]{2,1,0:T(8,128)(2,1)}), bf16[16,128,768]{2,1,0:T(8,128)(2,1)S(1)}, u32[]{:S(2)}, u32[]{:S(2)}) async-start(bf16[16,128,768]{2,1,0:T(8,128)(2,1)} %bitcast.47), calls=%async_computation.2 | async-start | bytes 6291456 | tf_op jit(solution)/shard_map/all_to_all | solution.py:84
